TPU v7x, 32 devices: a whole 2x2x4 slice. The times are simulated.
32 devices in a mesh: rows: 8 (over z, x), width: 4 (over y, core).
Axes of the slice: x: 2, y: 2, z: 4, core: 2. Of those that a mesh axis runs over, the one named last changes fastest.
Arguments:
- queries: bfloat16 [6144, 4096], P('rows', 'width')
- passages: bfloat16 [2048, 4096], P('rows', 'width')
- neighbor_ids: int32 [24, 4], P('rows'), may hold values from 0 to 7, as said below
- counts: int32 [24], P('rows'), may hold values from 1 to 4
Outputs:
- losses: float32 [6144], P(('rows', 'width'))
- grad_queries: bfloat16 [6144, 4096], P('rows', 'width')
- grad_passages: bfloat16 [2048, 4096], P('rows', 'width')
Inputs may be any that keep to these rules, and one draw needn't show every extreme that they name: `neighbor_ids`: entry k of row c, for k below counts[c], names a passage block one or two blocks away from block c // 3 in the cyclic order of 8 blocks, all different within the row; the remaining entries name block c // 3.
All inputs are finite; a program needn't handle non-finite values.
Results may differ from a plain program's by a relative error of at most 0.0049.
Values may be sent and summed in bfloat16 or wider, within the bound.
A program may use at most 64 MiB of HBM per device.

v0:
```python
import jax
import jax.numpy as jnp
from jax import lax
from jax.sharding import PartitionSpec as P

BLOCK = 256
inverse_sharpness_scale = 50.0


def passed_along(block, axis, distance):
    devices = range(lax.axis_size(axis))
    route = [((i - distance) % len(devices), i) for i in devices]
    return lax.ppermute(block, axis, route)


def block_mask(neighbor_rows, count_rows, owner, nblocks):
    listed = jnp.arange(neighbor_rows.shape[1], dtype=jnp.int32)[None, :] < count_rows[:, None]
    columns = []
    for offset in range(5):
        if offset == 2:
            columns.append(jnp.ones((neighbor_rows.shape[0],), dtype=bool))
        else:
            target = (owner + offset - 2 + nblocks) % nblocks
            columns.append(jnp.any(listed & (neighbor_rows == target), axis=1))
    return jnp.stack(columns, axis=1)


def score_grads(pairwise_logits, row_exists_flag, local_rows):
    width_block = pairwise_logits.shape[1] // 5
    column_mask = jnp.repeat(row_exists_flag, width_block, axis=1)
    masked = jnp.where(column_mask, pairwise_logits, -jnp.inf)
    row_max = jnp.max(masked, axis=1, keepdims=True)
    expon = jnp.exp(masked - row_max)
    row_sum = jnp.sum(expon, axis=1, keepdims=True)
    normalized_probability = expon / row_sum
    positive_col = 2 * width_block + local_rows % width_block
    matching_pair_mask = (
        jnp.arange(pairwise_logits.shape[1], dtype=jnp.int32)[None, :] == positive_col[:, None]
    )
    positive = jnp.sum(jnp.where(matching_pair_mask, pairwise_logits, 0.0), axis=1)
    losses = row_max[:, 0] + jnp.log(row_sum[:, 0]) - positive
    derivative_entries = (
        inverse_sharpness_scale * (normalized_probability - matching_pair_mask.astype(jnp.float32))
    ).astype(jnp.bfloat16)
    return (losses, derivative_entries)


def per_device(queries, passages, neighbor_ids, counts):
    nblocks = lax.axis_size("rows")
    owner = lax.axis_index("rows")
    per_dev = queries.shape[0]
    present = block_mask(neighbor_ids, counts, owner, nblocks)
    fetched = []
    for offset in range(5):
        if offset == 2:
            fetched.append(passages)
        else:
            fetched.append(passed_along(passages, "rows", 2 - offset))
    candidates = jnp.concatenate(fetched, axis=0)
    score_dims = (((1,), (1,)), ((), ()))
    quantity_proportion = lax.dot_general(
        queries, candidates, score_dims, preferred_element_type=jnp.float32
    )
    row_exists_flag = jnp.repeat(present, BLOCK, axis=0)
    share_rows = per_dev // lax.axis_size("width")
    share_start = lax.axis_index("width") * share_rows
    pairwise_logits = lax.psum(quantity_proportion, "width") * inverse_sharpness_scale
    all_losses, derivative_entries = score_grads(
        pairwise_logits, row_exists_flag, jnp.arange(per_dev, dtype=jnp.int32)
    )
    losses = lax.dynamic_slice_in_dim(all_losses, share_start, share_rows, 0)
    grad_q = jnp.dot(derivative_entries, candidates, preferred_element_type=jnp.float32)
    passage_terms = lax.dot_general(
        derivative_entries, queries, (((0,), (0,)), ((), ())), preferred_element_type=jnp.float32
    )
    term_sums = [passage_terms[offset * BLOCK : (offset + 1) * BLOCK] for offset in range(5)]
    total = term_sums[2]
    for offset in (0, 1, 3, 4):
        arrived = passed_along(term_sums[offset].astype(jnp.bfloat16), "rows", offset - 2)
        total = total + arrived.astype(jnp.float32)
    return (losses, grad_q.astype(jnp.bfloat16), total.astype(jnp.bfloat16))


def solution(mesh):
    return jax.shard_map(
        per_device,
        mesh=mesh,
        in_specs=(P("rows", "width"), P("rows", "width"), P("rows", None), P("rows")),
        out_specs=(P(("rows", "width")), P("rows", "width"), P("rows", "width")),
        check_vma=False,
    )
```

profile of v0, /device:TPU:0, one launch (start us, length us, event | category | flops | bytes accessed | tf_op | source)
XLA Modules:
  0.0 190.1 jit_solution(16085234565629834959)
XLA Ops:
  7.2 0.0 copy-start
  7.2 0.0 all-reduce.2.cloned.1.call-start
  7.2 3.1 %collective-permute-start = (bf16[256,1024]{1,0:T(8,128)(2,1)}, bf16[256,1024]{1,0:T(8,128)(2,1)S(1)}, u32[]{:S(2)}, u32[]{:S(2)}) collective-permute-start(bf16[256,1024]{1,0:T(8,128)(2,1)} %param.5), channel_id=1, source_target_pairs={{24,0},{28,4},{0,8},{4,12},{8,16},{12,20},{16,24},{20,28},{25,1},{... | collective-permute-start | bytes 1572872 | tf_op jit(solution)/shard_map/ppermute | solution.py:13
  10.3 1.5 collective-permute-start.1
  11.8 3.2 %collective-permute-start.2 = (bf16[256,1024]{1,0:T(8,128)(2,1)}, bf16[256,1024]{1,0:T(8,128)(2,1)S(1)}, u32[]{:S(2)}, u32[]{:S(2)}) collective-permute-start(bf16[256,1024]{1,0:T(8,128)(2,1)} %param.5), channel_id=1, source_target_pairs={{4,0},{8,4},{12,8},{16,12},{20,16},{24,20},{28,24},{0,28},{5,1},{9... | collective-permute-start | bytes 1572872 | tf_op jit(solution)/shard_map/ppermute | solution.py:13
  15.0 0.3 collective-permute-start.3
  15.3 10.0 %collective-permute-done = bf16[256,1024]{1,0:T(8,128)(2,1)S(1)} collective-permute-done((bf16[256,1024]{1,0:T(8,128)(2,1)}, bf16[256,1024]{1,0:T(8,128)(2,1)S(1)}, u32[]{:S(2)}, u32[]{:S(2)}) %collective-permute-start) | collective-permute-done | bytes 524320 | tf_op jit(solution)/shard_map/ppermute | solution.py:13
  25.4 12.4 %collective-permute-done.1 = bf16[256,1024]{1,0:T(8,128)(2,1)S(1)} collective-permute-done((bf16[256,1024]{1,0:T(8,128)(2,1)}, bf16[256,1024]{1,0:T(8,128)(2,1)S(1)}, u32[]{:S(2)}, u32[]{:S(2)}) %collective-permute-start.1) | collective-permute-done | bytes 524320 | tf_op jit(solution)/shard_map/ppermute | solution.py:13
  37.8 1.1 constant_dynamic-update-slice_fusion.2
  38.9 8.0 %collective-permute-done.3 = bf16[256,1024]{1,0:T(8,128)(2,1)S(1)} collective-permute-done((bf16[256,1024]{1,0:T(8,128)(2,1)}, bf16[256,1024]{1,0:T(8,128)(2,1)S(1)}, u32[]{:S(2)}, u32[]{:S(2)}) %collective-permute-start.3) | collective-permute-done | bytes 524320 | tf_op jit(solution)/shard_map/ppermute | solution.py:13
  47.0 1.6 copy-done.2
  48.5 4.1 %convolution_bitcast_fusion = f32[768,1280]{0,1:T(8,128)} fusion(bf16[1280,1024]{1,0:T(8,128)(2,1)S(1)} %constant_dynamic-update-slice_fusion, bf16[768,1024]{1,0:T(8,128)(2,1)S(1)} %copy-done), kind=kOutput, calls=%fused_computation.5 | convolution fusion | flops 2013265920 | bytes 8126464 | tf_op jit(solution)/shard_map/dot_general | solution.py:61
  52.7 0.0 all-reduce.2.cloned.1.call-update
  52.8 0.6 copy-done.4
  53.4 0.2 fusion.17
  53.6 0.1 broadcast_bitcast_fusion
  53.7 81.0 %all-reduce.2.cloned.1.call-done = f32[768,1280]{0,1:T(8,128)} async-done(((f32[768,1280]{0,1:T(8,128)}), f32[768,1280]{0,1:T(8,128)}) %all-reduce.2.cloned.1.call-update) | async-done | bytes 3932176 | tf_op jit(solution)/shard_map/psum | solution.py:67
  134.7 2.7 %fusion = f32[768]{0:T(1024)S(1)} fusion(f32[768,1280]{0,1:T(8,128)} %all-reduce.2.cloned.1.call-done, pred[768,5]{0,1:T(8,128)(4,1)S(1)} %bitcast.27), kind=kLoop, calls=%fused_computation.6 | loop fusion | flops 2948352 | bytes 3939072 | tf_op jit(solution)/shard_map/reduce_max | solution.py:32
  137.4 0.6 copy-done.1
  138.0 1.3 fusion.1
  139.3 1.5 multiply_convert_fusion
  140.8 2.2 %fusion.19 = (bf16[1280,1024]{1,0:T(8,128)(2,1)S(1)}, f32[1280,1024]{1,0:T(8,128)S(1)}) fusion(bf16[768,1280]{0,1:T(8,128)(2,1)S(1)} %multiply_convert_fusion, bf16[768,1024]{1,0:T(8,128)(2,1)S(1)} %copy-done), kind=kOutput, calls=%fused_computation.37 | convolution fusion | flops 2014576640 | bytes 11403264 | tf_op jit(solution)/shard_map/dot_general | solution.py:73
  143.0 0.2 fusion.18
  143.2 3.4 %collective-permute-start.4 = (bf16[256,1024]{1,0:T(8,128)(2,1)S(1)}, bf16[256,1024]{1,0:T(8,128)(2,1)S(1)}, u32[]{:S(2)}, u32[]{:S(2)}) collective-permute-start(bf16[256,1024]{1,0:T(8,128)(2,1)S(1)} %get-tuple-element.9), channel_id=1, source_target_pairs={{8,0},{12,4},{16,8},{20,12},{24,16},{28,20},{0,24},{4,28},{9,1},{1... | collective-permute-start | bytes 1572872 | tf_op jit(solution)/shard_map/ppermute | solution.py:13
  146.6 1.5 collective-permute-start.6
  148.1 3.3 %collective-permute-start.5 = (bf16[256,1024]{1,0:T(8,128)(2,1)S(1)}, bf16[256,1024]{1,0:T(8,128)(2,1)S(1)}, u32[]{:S(2)}, u32[]{:S(2)}) collective-permute-start(bf16[256,1024]{1,0:T(8,128)(2,1)S(1)} %get-tuple-element.12), channel_id=1, source_target_pairs={{4,0},{8,4},{12,8},{16,12},{20,16},{24,20},{28,24},{0,28},{5,1},{9... | collective-permute-start | bytes 1572872 | tf_op jit(solution)/shard_map/ppermute | solution.py:13
  151.3 0.6 dynamic_slice.3
  152.0 3.4 %convolution_convert_fusion = bf16[768,1024]{1,0:T(8,128)(2,1)} fusion(bf16[768,1280]{0,1:T(8,128)(2,1)S(1)} %multiply_convert_fusion, bf16[1280,1024]{1,0:T(8,128)(2,1)S(1)} %copy-done.3), kind=kOutput, calls=%fused_computation.8 | convolution fusion | flops 2014052352 | bytes 6160384 | tf_op jit(solution)/shard_map/dot_general | solution.py:72
  155.4 3.6 %collective-permute-done.4 = bf16[256,1024]{1,0:T(8,128)(2,1)S(1)} collective-permute-done((bf16[256,1024]{1,0:T(8,128)(2,1)S(1)}, bf16[256,1024]{1,0:T(8,128)(2,1)S(1)}, u32[]{:S(2)}, u32[]{:S(2)}) %collective-permute-start.4) | collective-permute-done | bytes 524320 | tf_op jit(solution)/shard_map/ppermute | solution.py:13
  158.9 12.3 %collective-permute-done.7 = bf16[256,1024]{1,0:T(8,128)(2,1)S(1)} collective-permute-done((bf16[256,1024]{1,0:T(8,128)(2,1)S(1)}, bf16[256,1024]{1,0:T(8,128)(2,1)S(1)}, u32[]{:S(2)}, u32[]{:S(2)}) %collective-permute-start.7) | collective-permute-done | bytes 524320 | tf_op jit(solution)/shard_map/ppermute | solution.py:13
  171.2 10.8 %collective-permute-done.6 = bf16[256,1024]{1,0:T(8,128)(2,1)S(1)} collective-permute-done((bf16[256,1024]{1,0:T(8,128)(2,1)S(1)}, bf16[256,1024]{1,0:T(8,128)(2,1)S(1)}, u32[]{:S(2)}, u32[]{:S(2)}) %collective-permute-start.6) | collective-permute-done | bytes 524320 | tf_op jit(solution)/shard_map/ppermute | solution.py:13
  182.0 1.3 fusion.5
  (20 shorter events, 0.2 us)
Async XLA Ops:
  7.2 41.4 %copy-start = (bf16[768,1024]{1,0:T(8,128)(2,1)S(1)}, bf16[768,1024]{1,0:T(8,128)(2,1)}, u32[]{:S(2)}) copy-start(bf16[768,1024]{1,0:T(8,128)(2,1)} %param.4) | copy-start | bytes 4718596
  7.2 127.5 %all-reduce.2.cloned.1.call-start = ((), (), s32[]{:S(2)}) async-start(), calls=%async_computation | async-start | bytes 7864320 | tf_op jit(solution)/shard_map/psum | solution.py:67
  7.2 18.1 %collective-permute-start = (bf16[256,1024]{1,0:T(8,128)(2,1)}, bf16[256,1024]{1,0:T(8,128)(2,1)S(1)}, u32[]{:S(2)}, u32[]{:S(2)}) collective-permute-start(bf16[256,1024]{1,0:T(8,128)(2,1)} %param.5), channel_id=1, source_target_pairs={{24,0},{28,4},{0,8},{4,12},{8,16},{12,20},{16,24},{20,28},{25,1},{... | collective-permute-start | bytes 1572872 | tf_op jit(solution)/shard_map/ppermute | solution.py:13
  10.3 27.4 %collective-permute-start.1 = (bf16[256,1024]{1,0:T(8,128)(2,1)}, bf16[256,1024]{1,0:T(8,128)(2,1)S(1)}, u32[]{:S(2)}, u32[]{:S(2)}) collective-permute-start(bf16[256,1024]{1,0:T(8,128)(2,1)} %param.5), channel_id=1, source_target_pairs={{28,0},{0,4},{4,8},{8,12},{12,16},{16,20},{20,24},{24,28},{29,1},{... | collective-permute-start | bytes 1572872 | tf_op jit(solution)/shard_map/ppermute | solution.py:13
  11.8 27.1 %collective-permute-start.2 = (bf16[256,1024]{1,0:T(8,128)(2,1)}, bf16[256,1024]{1,0:T(8,128)(2,1)S(1)}, u32[]{:S(2)}, u32[]{:S(2)}) collective-permute-start(bf16[256,1024]{1,0:T(8,128)(2,1)} %param.5), channel_id=1, source_target_pairs={{4,0},{8,4},{12,8},{16,12},{20,16},{24,20},{28,24},{0,28},{5,1},{9... | collective-permute-start | bytes 1572872 | tf_op jit(solution)/shard_map/ppermute | solution.py:13
  15.0 31.9 %collective-permute-start.3 = (bf16[256,1024]{1,0:T(8,128)(2,1)}, bf16[256,1024]{1,0:T(8,128)(2,1)S(1)}, u32[]{:S(2)}, u32[]{:S(2)}) collective-permute-start(bf16[256,1024]{1,0:T(8,128)(2,1)} %param.5), channel_id=1, source_target_pairs={{8,0},{12,4},{16,8},{20,12},{24,16},{28,20},{0,24},{4,28},{9,1},{1... | collective-permute-start | bytes 1572872 | tf_op jit(solution)/shard_map/ppermute | solution.py:13
  47.0 1.6 copy-start.2
  52.7 0.7 copy-start.4
  52.7 0.7 copy-start.5
  134.7 3.3 %copy-start.1 = (f32[768,1280]{0,1:T(8,128)S(1)}, f32[768,1280]{0,1:T(8,128)}, u32[]{:S(2)}) copy-start(f32[768,1280]{0,1:T(8,128)} %all-reduce.2.cloned.1.call-done) | copy-start | bytes 11796484
  143.0 8.9 %copy-start.3 = (bf16[1280,1024]{1,0:T(8,128)(2,1)S(1)}, bf16[1280,1024]{1,0:T(8,128)(2,1)}, u32[]{:S(2)}) copy-start(bf16[1280,1024]{1,0:T(8,128)(2,1)} %copy-done.2) | copy-start | bytes 7864324
  143.2 15.7 %collective-permute-start.4 = (bf16[256,1024]{1,0:T(8,128)(2,1)S(1)}, bf16[256,1024]{1,0:T(8,128)(2,1)S(1)}, u32[]{:S(2)}, u32[]{:S(2)}) collective-permute-start(bf16[256,1024]{1,0:T(8,128)(2,1)S(1)} %get-tuple-element.9), channel_id=1, source_target_pairs={{8,0},{12,4},{16,8},{20,12},{24,16},{28,20},{0,24},{4,28},{9,1},{1... | collective-permute-start | bytes 1572872 | tf_op jit(solution)/shard_map/ppermute | solution.py:13
  146.6 24.6 %collective-permute-start.7 = (bf16[256,1024]{1,0:T(8,128)(2,1)S(1)}, bf16[256,1024]{1,0:T(8,128)(2,1)S(1)}, u32[]{:S(2)}, u32[]{:S(2)}) collective-permute-start(bf16[256,1024]{1,0:T(8,128)(2,1)S(1)} %get-tuple-element.10), channel_id=1, source_target_pairs={{24,0},{28,4},{0,8},{4,12},{8,16},{12,20},{16,24},{20,28},{25,1},{... | collective-permute-start | bytes 1572872 | tf_op jit(solution)/shard_map/ppermute | solution.py:13
  146.6 35.4 %collective-permute-start.6 = (bf16[256,1024]{1,0:T(8,128)(2,1)S(1)}, bf16[256,1024]{1,0:T(8,128)(2,1)S(1)}, u32[]{:S(2)}, u32[]{:S(2)}) collective-permute-start(bf16[256,1024]{1,0:T(8,128)(2,1)S(1)} %get-tuple-element.11), channel_id=1, source_target_pairs={{28,0},{0,4},{4,8},{8,12},{12,16},{16,20},{20,24},{24,28},{29,1},{... | collective-permute-start | bytes 1572872 | tf_op jit(solution)/shard_map/ppermute | solution.py:13
  148.1 33.9 %collective-permute-start.5 = (bf16[256,1024]{1,0:T(8,128)(2,1)S(1)}, bf16[256,1024]{1,0:T(8,128)(2,1)S(1)}, u32[]{:S(2)}, u32[]{:S(2)}) collective-permute-start(bf16[256,1024]{1,0:T(8,128)(2,1)S(1)} %get-tuple-element.12), channel_id=1, source_target_pairs={{4,0},{8,4},{12,8},{16,12},{20,16},{24,20},{28,24},{0,28},{5,1},{9... | collective-permute-start | bytes 1572872 | tf_op jit(solution)/shard_map/ppermute | solution.py:13
Sparse Core Ops, SparseCore 0:
  52.8 81.8 all-reduce.1
where the time goes:
time: 190 us
  waiting for transfers between devices  138 us (73%)
  starting transfers between devices  16.2 us (9%)
  between operations  14.2 us (7%)
  matrix products  9.76 us (5%)
  other arithmetic  6.98 us (4%)
  local copies, waits for them, and re-layouts  4.91 us (3%)
    psum x1, waiting for transfers between devices, per_device(): lax.psum(quantity_proportion, 'width') * inverse_sharpness_scale  81 us
    ppermute x8, waiting for transfers between devices, passed_along(): return lax.ppermute(block, axis, route)  57 us
    ppermute x8, starting transfers between devices, passed_along(): return lax.ppermute(block, axis, route)  16.2 us
    dot_general x1, matrix products, per_device(): lax.dot_general(queries, candidates, score_dims, preferred_element_type=j...  4.15 us
    unnamed x18, local copies, waits for them, and re-layouts  4.03 us
  transfers between devices with their start and end apart: 9, of which 7 were waited for; matrix products, arithmetic and copies ran while one was open for 3% of the time, Pallas kernels for 0%

commit v1 on v0

--- a/solution.py
+++ b/solution.py
@@ -5,6 +5,12 @@
 
 BLOCK = 256
 inverse_sharpness_scale = 50.0
+
+
+def summed_here(x, axis):
+    blocks = lax.all_gather(x, axis, axis=0, tiled=False)
+    summed = blocks.sum(axis=0)
+    return summed
 
 
 def passed_along(block, axis, distance):
@@ -64,7 +70,7 @@
     row_exists_flag = jnp.repeat(present, BLOCK, axis=0)
     share_rows = per_dev // lax.axis_size("width")
     share_start = lax.axis_index("width") * share_rows
-    pairwise_logits = lax.psum(quantity_proportion, "width") * inverse_sharpness_scale
+    pairwise_logits = summed_here(quantity_proportion, "width") * inverse_sharpness_scale
     all_losses, derivative_entries = score_grads(
         pairwise_logits, row_exists_flag, jnp.arange(per_dev, dtype=jnp.int32)
     )

time: 190 us -> 243 us (1.28)
  waiting for transfers between devices: 138 us -> 158 us
  local copies, waits for them, and re-layouts: 4.91 us -> 24.5 us
  other arithmetic: 6.98 us -> 21.2 us
    all_gather x0 -> x1, waiting for transfers between devices: none -> 99.7 us  [summed_here(): blocks = lax.all_gather(x, axis, axis=0, tiled=False)]
    psum x1 -> x0, waiting for transfers between devices: 81 us -> none  [per_device(): lax.psum(quantity_proportion, 'width') * inverse_sharpness_scale]
    all_gather x0 -> x1, local copies, waits for them, and re-layouts: none -> 19.7 us  [summed_here(): blocks = lax.all_gather(x, axis, axis=0, tiled=False)]
    reduce_sum x0 -> x1, other arithmetic: none -> 14.2 us  [summed_here(): summed = blocks.sum(axis=0)]
  transfers between devices with their start and end apart: 9 -> 9, of which waited for: 7 -> 7; matrix products, arithmetic and copies ran while one was open for 3% -> 2% of each run, Pallas kernels for 0% -> 0%
where the time goes in v1:
time: 243 us; the launch traced here: 242 us
  waiting for transfers between devices  158 us (65%)
  local copies, waits for them, and re-layouts  24.5 us (10%)
  other arithmetic  21.2 us (9%)
  starting transfers between devices  14.9 us (6%)
  between operations  14.2 us (6%)
  matrix products  9.76 us (4%)
    all_gather x1, waiting for transfers between devices, summed_here(): blocks = lax.all_gather(x, axis, axis=0, tiled=False)  99.7 us
    ppermute x8, waiting for transfers between devices, passed_along(): return lax.ppermute(block, axis, route)  58 us
    all_gather x1, local copies, waits for them, and re-layouts, summed_here(): blocks = lax.all_gather(x, axis, axis=0, tiled=False)  19.7 us
    ppermute x8, starting transfers between devices, passed_along(): return lax.ppermute(block, axis, route)  14.9 us
    reduce_sum x1, other arithmetic, summed_here(): summed = blocks.sum(axis=0)  14.2 us
  transfers between devices with their start and end apart: 9, of which 7 were waited for; matrix products, arithmetic and copies ran while one was open for 2% of the time, Pallas kernels for 0%

profile of v1, /device:TPU:0, one launch (start us, length us, event | category | flops | bytes accessed | tf_op | source)
XLA Modules:
  0.0 242.3 jit_solution(15605843095708447844)
XLA Ops:
  7.2 3.1 %collective-permute-start = (bf16[256,1024]{1,0:T(8,128)(2,1)}, bf16[256,1024]{1,0:T(8,128)(2,1)S(1)}, u32[]{:S(2)}, u32[]{:S(2)}) collective-permute-start(bf16[256,1024]{1,0:T(8,128)(2,1)} %param.5), channel_id=1, source_target_pairs={{24,0},{28,4},{0,8},{4,12},{8,16},{12,20},{16,24},{20,28},{25,1},{... | collective-permute-start | bytes 1572872 | tf_op jit(solution)/shard_map/ppermute | solution.py:19
  10.3 1.5 collective-permute-start.1
  11.8 3.2 %collective-permute-start.2 = (bf16[256,1024]{1,0:T(8,128)(2,1)}, bf16[256,1024]{1,0:T(8,128)(2,1)S(1)}, u32[]{:S(2)}, u32[]{:S(2)}) collective-permute-start(bf16[256,1024]{1,0:T(8,128)(2,1)} %param.5), channel_id=1, source_target_pairs={{4,0},{8,4},{12,8},{16,12},{20,16},{24,20},{28,24},{0,28},{5,1},{9... | collective-permute-start | bytes 1572872 | tf_op jit(solution)/shard_map/ppermute | solution.py:19
  15.0 0.3 collective-permute-start.3
  15.3 10.0 %collective-permute-done = bf16[256,1024]{1,0:T(8,128)(2,1)S(1)} collective-permute-done((bf16[256,1024]{1,0:T(8,128)(2,1)}, bf16[256,1024]{1,0:T(8,128)(2,1)S(1)}, u32[]{:S(2)}, u32[]{:S(2)}) %collective-permute-start) | collective-permute-done | bytes 524320 | tf_op jit(solution)/shard_map/ppermute | solution.py:19
  25.4 12.4 %collective-permute-done.1 = bf16[256,1024]{1,0:T(8,128)(2,1)S(1)} collective-permute-done((bf16[256,1024]{1,0:T(8,128)(2,1)}, bf16[256,1024]{1,0:T(8,128)(2,1)S(1)}, u32[]{:S(2)}, u32[]{:S(2)}) %collective-permute-start.1) | collective-permute-done | bytes 524320 | tf_op jit(solution)/shard_map/ppermute | solution.py:19
  37.8 1.1 constant_dynamic-update-slice_fusion.2
  38.9 8.0 %collective-permute-done.3 = bf16[256,1024]{1,0:T(8,128)(2,1)S(1)} collective-permute-done((bf16[256,1024]{1,0:T(8,128)(2,1)}, bf16[256,1024]{1,0:T(8,128)(2,1)S(1)}, u32[]{:S(2)}, u32[]{:S(2)}) %collective-permute-start.3) | collective-permute-done | bytes 524320 | tf_op jit(solution)/shard_map/ppermute | solution.py:19
  47.0 1.5 copy-done.2
  48.4 4.1 %convolution_bitcast_fusion = f32[768,1280]{0,1:T(8,128)} fusion(bf16[1280,1024]{1,0:T(8,128)(2,1)S(1)} %constant_dynamic-update-slice_fusion, bf16[768,1024]{1,0:T(8,128)(2,1)S(1)} %copy-done), kind=kOutput, calls=%fused_computation.5 | convolution fusion | flops 2013265920 | bytes 8126464 | tf_op jit(solution)/shard_map/dot_general | solution.py:67
  52.7 0.6 copy-done.4
  53.3 0.2 fusion.17
  53.5 0.1 broadcast_bitcast_fusion
  53.6 99.7 %all-gather.3.cloned.1.call-done = f32[3072,1280]{0,1:T(8,128)} async-done(((f32[768,1280]{0,1:T(8,128)}), f32[3072,1280]{0,1:T(8,128)}) %all-gather.3.cloned.1.call-update) | async-done | bytes 15728656 | tf_op jit(solution)/shard_map/all_gather | solution.py:11
  153.4 19.7 %reshape.41 = f32[4,768,1280]{1,0,2:T(4,128)} reshape(f32[3072,1280]{0,1:T(8,128)} %all-gather.3.cloned.1.call-done) | data formatting | bytes 31457280 | tf_op jit(solution)/shard_map/all_gather | solution.py:11
  173.1 14.2 %reduce_sum.27 = f32[768,1280]{0,1:T(8,128)} reduce(f32[4,768,1280]{1,0,2:T(4,128)} %reshape.41, f32[]{:T(128)} %constant.75.clone.1), dimensions={0}, to_apply=%region_4.5 | reduce | flops 2949120 | bytes 19660804 | tf_op jit(solution)/shard_map/reduce_sum | solution.py:12
  187.3 2.7 %fusion = f32[768]{0:T(1024)S(1)} fusion(f32[768,1280]{0,1:T(8,128)} %reduce_sum.27, pred[768,5]{0,1:T(8,128)(4,1)S(1)} %bitcast.29), kind=kLoop, calls=%fused_computation.6 | loop fusion | flops 2948352 | bytes 3939072 | tf_op jit(solution)/shard_map/reduce_max | solution.py:38
  190.1 0.6 copy-done.1
  190.6 1.3 fusion.1
  191.9 1.5 multiply_convert_fusion
  193.4 2.2 fusion.19
  195.6 0.2 fusion.18
  195.8 1.5 collective-permute-start.7
  197.3 1.5 collective-permute-start.6
  198.8 3.3 %collective-permute-start.5 = (bf16[256,1024]{1,0:T(8,128)(2,1)S(1)}, bf16[256,1024]{1,0:T(8,128)(2,1)S(1)}, u32[]{:S(2)}, u32[]{:S(2)}) collective-permute-start(bf16[256,1024]{1,0:T(8,128)(2,1)S(1)} %get-tuple-element.12), channel_id=1, source_target_pairs={{4,0},{8,4},{12,8},{16,12},{20,16},{24,20},{28,24},{0,28},{5,1},{9... | collective-permute-start | bytes 1572872 | tf_op jit(solution)/shard_map/ppermute | solution.py:19
  202.1 0.5 collective-permute-start.4
  202.6 0.6 dynamic_slice.3
  203.2 3.4 %convolution_convert_fusion = bf16[768,1024]{1,0:T(8,128)(2,1)} fusion(bf16[768,1280]{0,1:T(8,128)(2,1)S(1)} %multiply_convert_fusion, bf16[1280,1024]{1,0:T(8,128)(2,1)S(1)} %copy-done.3), kind=kOutput, calls=%fused_computation.8 | convolution fusion | flops 2014052352 | bytes 6160384 | tf_op jit(solution)/shard_map/dot_general | solution.py:78
  206.7 5.8 %collective-permute-done.7 = bf16[256,1024]{1,0:T(8,128)(2,1)S(1)} collective-permute-done((bf16[256,1024]{1,0:T(8,128)(2,1)S(1)}, bf16[256,1024]{1,0:T(8,128)(2,1)S(1)}, u32[]{:S(2)}, u32[]{:S(2)}) %collective-permute-start.7) | collective-permute-done | bytes 524320 | tf_op jit(solution)/shard_map/ppermute | solution.py:19
  212.5 12.1 %collective-permute-done.6 = bf16[256,1024]{1,0:T(8,128)(2,1)S(1)} collective-permute-done((bf16[256,1024]{1,0:T(8,128)(2,1)S(1)}, bf16[256,1024]{1,0:T(8,128)(2,1)S(1)}, u32[]{:S(2)}, u32[]{:S(2)}) %collective-permute-start.6) | collective-permute-done | bytes 524320 | tf_op jit(solution)/shard_map/ppermute | solution.py:19
  224.6 9.6 %collective-permute-done.4 = bf16[256,1024]{1,0:T(8,128)(2,1)S(1)} collective-permute-done((bf16[256,1024]{1,0:T(8,128)(2,1)S(1)}, bf16[256,1024]{1,0:T(8,128)(2,1)S(1)}, u32[]{:S(2)}, u32[]{:S(2)}) %collective-permute-start.4) | collective-permute-done | bytes 524320 | tf_op jit(solution)/shard_map/ppermute | solution.py:19
  234.2 1.3 fusion.5
  (22 shorter events, 0.3 us)
Async XLA Ops:
  7.2 41.3 %copy-start = (bf16[768,1024]{1,0:T(8,128)(2,1)S(1)}, bf16[768,1024]{1,0:T(8,128)(2,1)}, u32[]{:S(2)}) copy-start(bf16[768,1024]{1,0:T(8,128)(2,1)} %param.4) | copy-start | bytes 4718596
  7.2 146.2 %all-gather.3.cloned.1.call-start = ((), (), s32[]{:S(2)}) async-start(), calls=%async_computation | async-start | bytes 19660800 | tf_op jit(solution)/shard_map/all_gather | solution.py:11
  7.2 18.1 %collective-permute-start = (bf16[256,1024]{1,0:T(8,128)(2,1)}, bf16[256,1024]{1,0:T(8,128)(2,1)S(1)}, u32[]{:S(2)}, u32[]{:S(2)}) collective-permute-start(bf16[256,1024]{1,0:T(8,128)(2,1)} %param.5), channel_id=1, source_target_pairs={{24,0},{28,4},{0,8},{4,12},{8,16},{12,20},{16,24},{20,28},{25,1},{... | collective-permute-start | bytes 1572872 | tf_op jit(solution)/shard_map/ppermute | solution.py:19
  10.3 27.4 %collective-permute-start.1 = (bf16[256,1024]{1,0:T(8,128)(2,1)}, bf16[256,1024]{1,0:T(8,128)(2,1)S(1)}, u32[]{:S(2)}, u32[]{:S(2)}) collective-permute-start(bf16[256,1024]{1,0:T(8,128)(2,1)} %param.5), channel_id=1, source_target_pairs={{28,0},{0,4},{4,8},{8,12},{12,16},{16,20},{20,24},{24,28},{29,1},{... | collective-permute-start | bytes 1572872 | tf_op jit(solution)/shard_map/ppermute | solution.py:19
  11.8 27.1 %collective-permute-start.2 = (bf16[256,1024]{1,0:T(8,128)(2,1)}, bf16[256,1024]{1,0:T(8,128)(2,1)S(1)}, u32[]{:S(2)}, u32[]{:S(2)}) collective-permute-start(bf16[256,1024]{1,0:T(8,128)(2,1)} %param.5), channel_id=1, source_target_pairs={{4,0},{8,4},{12,8},{16,12},{20,16},{24,20},{28,24},{0,28},{5,1},{9... | collective-permute-start | bytes 1572872 | tf_op jit(solution)/shard_map/ppermute | solution.py:19
  15.0 31.9 %collective-permute-start.3 = (bf16[256,1024]{1,0:T(8,128)(2,1)}, bf16[256,1024]{1,0:T(8,128)(2,1)S(1)}, u32[]{:S(2)}, u32[]{:S(2)}) collective-permute-start(bf16[256,1024]{1,0:T(8,128)(2,1)} %param.5), channel_id=1, source_target_pairs={{8,0},{12,4},{16,8},{20,12},{24,16},{28,20},{0,24},{4,28},{9,1},{1... | collective-permute-start | bytes 1572872 | tf_op jit(solution)/shard_map/ppermute | solution.py:19
  47.0 1.5 copy-start.2
  52.6 0.7 copy-start.4
  52.6 0.7 copy-start.5
  187.3 3.3 %copy-start.1 = (f32[768,1280]{0,1:T(8,128)S(1)}, f32[768,1280]{0,1:T(8,128)}, u32[]{:S(2)}) copy-start(f32[768,1280]{0,1:T(8,128)} %reduce_sum.27) | copy-start | bytes 11796484
  195.6 7.6 %copy-start.3 = (bf16[1280,1024]{1,0:T(8,128)(2,1)S(1)}, bf16[1280,1024]{1,0:T(8,128)(2,1)}, u32[]{:S(2)}) copy-start(bf16[1280,1024]{1,0:T(8,128)(2,1)} %copy-done.2) | copy-start | bytes 7864324
  195.8 16.6 %collective-permute-start.7 = (bf16[256,1024]{1,0:T(8,128)(2,1)S(1)}, bf16[256,1024]{1,0:T(8,128)(2,1)S(1)}, u32[]{:S(2)}, u32[]{:S(2)}) collective-permute-start(bf16[256,1024]{1,0:T(8,128)(2,1)S(1)} %get-tuple-element.10), channel_id=1, source_target_pairs={{24,0},{28,4},{0,8},{4,12},{8,16},{12,20},{16,24},{20,28},{25,1},{... | collective-permute-start | bytes 1572872 | tf_op jit(solution)/shard_map/ppermute | solution.py:19
  197.3 27.2 %collective-permute-start.6 = (bf16[256,1024]{1,0:T(8,128)(2,1)S(1)}, bf16[256,1024]{1,0:T(8,128)(2,1)S(1)}, u32[]{:S(2)}, u32[]{:S(2)}) collective-permute-start(bf16[256,1024]{1,0:T(8,128)(2,1)S(1)} %get-tuple-element.11), channel_id=1, source_target_pairs={{28,0},{0,4},{4,8},{8,12},{12,16},{16,20},{20,24},{24,28},{29,1},{... | collective-permute-start | bytes 1572872 | tf_op jit(solution)/shard_map/ppermute | solution.py:19
  198.8 25.8 %collective-permute-start.5 = (bf16[256,1024]{1,0:T(8,128)(2,1)S(1)}, bf16[256,1024]{1,0:T(8,128)(2,1)S(1)}, u32[]{:S(2)}, u32[]{:S(2)}) collective-permute-start(bf16[256,1024]{1,0:T(8,128)(2,1)S(1)} %get-tuple-element.12), channel_id=1, source_target_pairs={{4,0},{8,4},{12,8},{16,12},{20,16},{24,20},{28,24},{0,28},{5,1},{9... | collective-permute-start | bytes 1572872 | tf_op jit(solution)/shard_map/ppermute | solution.py:19
  202.1 32.1 %collective-permute-start.4 = (bf16[256,1024]{1,0:T(8,128)(2,1)S(1)}, bf16[256,1024]{1,0:T(8,128)(2,1)S(1)}, u32[]{:S(2)}, u32[]{:S(2)}) collective-permute-start(bf16[256,1024]{1,0:T(8,128)(2,1)S(1)} %get-tuple-element.9), channel_id=1, source_target_pairs={{8,0},{12,4},{16,8},{20,12},{24,16},{28,20},{0,24},{4,28},{9,1},{1... | collective-permute-start | bytes 1572872 | tf_op jit(solution)/shard_map/ppermute | solution.py:19
Sparse Core Ops, SparseCore 0:
  52.7 100.5 all-gather.2
